TPU v7x, 128 devices: a whole 4x4x4 slice. The times are simulated.
128 devices in a mesh: ctx: 8 (over y_hi, x), exp: 16 (over y_lo, z, core).
Axes of the slice: x: 4, y: 4 (y_hi: 2, y_lo: 2; y = y_hi * 2 + y_lo), z: 4, core: 2. Of those that a mesh axis runs over, the one named last changes fastest.
Arguments:
- queries: bfloat16 [16, 1024, 2048], P('exp', 'ctx'), may hold values from -6 to 6
- key_rows: bfloat16 [16, 1024, 256], P('exp', 'ctx'), may hold values from -6 to 6
- value_matrix: bfloat16 [16, 1024, 256], P('exp', 'ctx'), may hold values from -4 to 4
- hidden: bfloat16 [16, 1024, 2880], P('exp', 'ctx'), may hold values from -30 to 30
- out_weight: bfloat16 [2048, 2880], P('ctx'), may hold values from -0.125 to 0.125
- norm_gain: float32 [2880], replicated, may hold values from 0.1 to 1.9
- block_order: int32 [16], replicated, may hold values from 0 to 15, each once
- expert_ids: int32 [16, 1024, 4], P('exp', 'ctx'), may hold values from 0 to 63, all different within a row; in each aligned block of 128 rows (0 to 127, 128 to 255, ..., all dimensions but the last counted through in order) at most 16 rows name the same one
- route_weights: float32 [16, 1024, 4], P('exp', 'ctx'), may hold values from 0.1 to 0.6
- gate_up_weight: bfloat16 [128, 2880, 1440], P(('ctx', 'exp')), may hold values from -0.109375 to 0.109375
- down_weight: bfloat16 [128, 720, 2880], P(('ctx', 'exp')), may hold values from -0.15625 to 0.15625
Outputs:
- layer_out: bfloat16 [16, 1024, 2880], P('exp', 'ctx')
Inputs may be any that keep to these rules, and one draw needn't show every extreme that they name: `expert_ids`: the 128 rows of one device (aligned blocks of rows) name any one expert at most 16 times, a bound that some block reaches.
All inputs are finite; a program needn't handle non-finite values.
Results may differ from a plain program's by a relative error of at most 0.017.
Values may be sent and summed in bfloat16 or wider, within the bound.
A program may use at most 128 MiB of HBM per device.

v0:
```python
import jax
import jax.numpy as jnp
from jax import lax
from jax.sharding import Mesh, PartitionSpec as P

D = 2880
QUERY_HEADS = 32
KEY_VALUE_HEADS = 4
HEAD_SIZE = 64
TOPK = 4
EXPERTS = 64
CAP = 16
CTX = ("y_hi", "x")
EXP = ("y_lo", "z", "core")
CHIPS = ("y_hi", "x", "y_lo", "z")
negative_large = -1e30


def attention(queries, key_rows, value_matrix, block_order):
    token_count = queries.shape[1]
    block_len = token_count // 2
    group = QUERY_HEADS // KEY_VALUE_HEADS
    slot_ids = jnp.arange(16, dtype=jnp.int32)

    def locate(row_index):
        table = (row_index // block_len)[:, None] == slot_ids[None, :]
        return (
            jnp.sum(jnp.where(table, block_order[None, :], 0), axis=1) * block_len
            + row_index % block_len
        )

    query_pos = locate(lax.axis_index(CTX) * token_count + jnp.arange(token_count, dtype=jnp.int32))
    query_head_rows = queries[0].reshape(token_count, KEY_VALUE_HEADS, group, HEAD_SIZE)
    both = lax.all_gather(
        jnp.concatenate([key_rows[0], value_matrix[0]], axis=1), CTX, axis=0, tiled=True
    )
    section_length = both.shape[0]
    key_pos = locate(jnp.arange(section_length, dtype=jnp.int32))
    kv = both.reshape(section_length, 2, KEY_VALUE_HEADS, HEAD_SIZE)
    key_head_rows, value_head_rows = (kv[:, 0], kv[:, 1])
    scores = jnp.einsum(
        "qhgd,khd->hgqk", query_head_rows, key_head_rows, preferred_element_type=jnp.float32
    ) * HEAD_SIZE ** (-0.5)
    visible = key_pos[None, :] <= query_pos[:, None]
    masked = jnp.where(visible, scores, negative_large)
    new_max = jnp.max(masked, axis=-1)
    kept_probs = jnp.where(visible, jnp.exp(masked - new_max[..., None]), 0.0)
    row_total = jnp.sum(kept_probs, axis=-1)
    added = jnp.einsum(
        "hgqk,khd->qhgd",
        kept_probs.astype(jnp.bfloat16),
        value_head_rows,
        preferred_element_type=jnp.float32,
    )
    return (
        (added / jnp.transpose(row_total, (2, 0, 1))[..., None])
        .astype(jnp.bfloat16)
        .reshape(token_count, QUERY_HEADS * HEAD_SIZE)
    )


def local(
    queries,
    key_rows,
    value_matrix,
    hidden,
    out_weight,
    norm_gain,
    block_order,
    expert_ids,
    route_weights,
    gate_up_weight,
    down_weight,
):
    swap = [(0, 1), (1, 0)]
    gate_up_own, down_own = (gate_up_weight[0], down_weight[0])
    gate_up_oth = lax.ppermute(gate_up_own, "core", swap)
    down_oth = lax.ppermute(down_own, "core", swap)
    attended = attention(queries, key_rows, value_matrix, block_order)
    projected = jnp.dot(
        attended,
        lax.all_gather(out_weight, CTX, axis=0, tiled=True),
        preferred_element_type=jnp.float32,
    )
    residual = (hidden[0].astype(jnp.float32) + projected).astype(jnp.bfloat16)
    res_float = residual.astype(jnp.float32)
    moe_in = (
        res_float
        * lax.rsqrt(jnp.mean(res_float * res_float, axis=-1, keepdims=True) + 1e-05)
        * norm_gain
    ).astype(jnp.bfloat16)
    ids, weights = (expert_ids[0], route_weights[0])
    token_count = ids.shape[0]
    named = ids[:, :, None] == jnp.arange(EXPERTS, dtype=jnp.int32)
    member = jnp.any(named, axis=1)
    weight_of = jnp.sum(jnp.where(named, weights[:, :, None], 0.0), axis=1)
    tok = jnp.arange(token_count, dtype=jnp.int32)
    before = (tok[None, :] < tok[:, None]).astype(jnp.bfloat16)
    slot = jnp.dot(before, member.astype(jnp.bfloat16), preferred_element_type=jnp.float32).astype(
        jnp.int32
    )
    place = (
        member.T[:, None, :]
        & (slot.T[:, None, :] == jnp.arange(CAP, dtype=jnp.int32)[None, :, None])
    ).reshape(EXPERTS * CAP, token_count)
    picked = place.astype(jnp.bfloat16)
    spread = jnp.where(
        place,
        jnp.broadcast_to(weight_of.T[:, None, :], (EXPERTS, CAP, token_count)).reshape(
            EXPERTS * CAP, token_count
        ),
        0.0,
    )
    high = spread.astype(jnp.bfloat16)
    low = (spread - high.astype(jnp.float32)).astype(jnp.bfloat16)
    outgoing = jnp.dot(picked, moe_in, preferred_element_type=jnp.float32).astype(jnp.bfloat16)
    rows = lax.all_to_all(
        outgoing.reshape(EXPERTS, CAP, D), CHIPS, split_axis=0, concat_axis=0, tiled=True
    ).reshape(EXPERTS * CAP, D)

    def half(gate_up, down):
        gate_up_out = jnp.dot(rows, gate_up, preferred_element_type=jnp.float32)
        n = gate_up.shape[1] // 2
        gate, up = (gate_up_out[:, :n], gate_up_out[:, n:])
        act = (gate * jax.nn.sigmoid(1.702 * gate) * (up + 1.0)).astype(jnp.bfloat16)
        return jnp.dot(act, down, preferred_element_type=jnp.float32)

    result = (half(gate_up_own, down_own) + half(gate_up_oth, down_oth)).astype(jnp.bfloat16)
    returned = lax.all_to_all(
        result.reshape(EXPERTS, CAP, D), CHIPS, split_axis=0, concat_axis=0, tiled=True
    ).reshape(EXPERTS * CAP, D)
    mixed = jnp.einsum(
        "st,sd->td", high, returned, preferred_element_type=jnp.float32
    ) + jnp.einsum("st,sd->td", low, returned, preferred_element_type=jnp.float32)
    return (res_float + mixed).astype(jnp.bfloat16)[None]


def solution(mesh):
    fine = Mesh(mesh.devices.reshape(2, 4, 2, 4, 2), ("y_hi", "x", "y_lo", "z", "core"))
    rows = P(EXP, CTX, None)
    halves = P(CTX + EXP, None, None)
    return jax.shard_map(
        local,
        mesh=fine,
        in_specs=(rows, rows, rows, rows, P(CTX, None), P(), P(), rows, rows, halves, halves),
        out_specs=rows,
        check_vma=False,
    )
```

profile of v0, /device:TPU:98, one launch (start us, length us, event | category | flops | bytes accessed | tf_op | source)
XLA Modules:
  0.0 508.8 jit_solution(10034185863048073438)
XLA Ops:
  6.5 1.5 pad_maximum_fusion
  8.9 1.3 copy.36
  10.3 0.7 fusion.50
  11.4 0.7 select_reduce_fusion.2
  12.1 0.7 select_reduce_fusion.1
  13.1 45.0 %all-gather.3.cloned.1.call-done = bf16[1024,512]{1,0:T(8,128)(2,1)} async-done(((bf16[128,512]{1,0:T(8,128)(2,1)}), bf16[1024,512]{1,0:T(8,128)(2,1)}) %all-gather.3.cloned.1.call-update) | async-done | bytes 1048592 | tf_op jit(solution)/shard_map/all_gather | solution.py:34
  58.1 1.5 copy.35
  59.5 9.5 %fusion.71 = (f32[4,8,128]{2,1,0:T(8,128)S(1)}, bf16[4,8,128,1024]{2,3,1,0:T(8,128)(2,1)}) fusion(pred[128,1024]{0,1:T(8,128)(4,1)S(1)} %broadcast_compare_fusion, bf16[128,4,8,64]{0,3,2,1:T(8,128)(2,1)S(1)} %bitcast.97, bf16[1024,2,4,64]{0,3,2,1:T(8,128)(2,1)S(1)} %bitcast.95), kind=kOutput, calls=%fused_computation.99 | convolution fusion | flops 562037760 | bytes 9715712 | tf_op jit(solution)/shard_map/sub | solution.py:47
  69.1 5.7 %fusion.32 = bf16[128,4,8,64]{0,3,2,1:T(8,128)(2,1)S(1)} fusion(bf16[4,8,128,1024]{2,3,1,0:T(8,128)(2,1)} %get-tuple-element.6, bf16[1024,2,4,64]{0,3,2,1:T(8,128)(2,1)S(1)} %bitcast.96, f32[128,4,8]{0,2,1:T(8,128)S(1)} %bitcast.111), kind=kOutput, calls=%fused_computation.36 | convolution fusion | flops 537395200 | bytes 9453568 | tf_op jit(solution)/shard_map/hgqk,khd->qhgd/dot_general | solution.py:49
  74.8 139.6 %all-gather.5.cloned.1.call-done = bf16[2048,2880]{0,1:T(8,128)(2,1)} async-done(((bf16[256,2880]{0,1:T(8,128)(2,1)}), bf16[2048,2880]{0,1:T(8,128)(2,1)}) %all-gather.5.cloned.1.call-update) | async-done | bytes 11796496 | tf_op jit(solution)/shard_map/all_gather | solution.py:82
  214.3 6.2 %multiply_reduce_fusion = (f32[128]{0:T(128)S(1)}, f32[128,2880]{0,1:T(8,128)S(1)}) fusion(bf16[2048,2880]{0,1:T(8,128)(2,1)} %all-gather.5.cloned.1.call-done, bf16[128,2048]{0,1:T(8,128)(2,1)S(1)} %bitcast.110, bf16[1,128,2880]{1,2,0:T(8,128)(2,1)S(1)} %copy-done.3), kind=kOutput, calls=%fused_computation.33 | convolution fusion | flops 1512161152 | bytes 14533120 | tf_op jit(solution)/shard_map/dot_general | solution.py:80
  220.5 4.0 convolution_convert_fusion
  224.5 8.5 %copy.38 = bf16[1024,2880]{1,0:T(8,128)(2,1)} copy(bf16[1024,2880]{0,1:T(8,128)(2,1)} %convolution_convert_fusion) | data formatting | bytes 11796480 | tf_op jit(solution)/shard_map/convert_element_type | solution.py:116
  233.1 8.2 %all-to-all-start = ((bf16[64,16,2880]{2,1,0:T(8,128)(2,1)}), bf16[64,16,2880]{2,1,0:T(8,128)(2,1)}, u32[]{:S(2)}, u32[]{:S(2)}) async-start(bf16[64,16,2880]{2,1,0:T(8,128)(2,1)} %bitcast.93), calls=%async_computation | async-start | bytes 12058624 | tf_op jit(solution)/shard_map/all_to_all | solution.py:117
  241.8 88.9 %all-to-all-done = bf16[64,16,2880]{2,1,0:T(8,128)(2,1)} async-done(((bf16[64,16,2880]{2,1,0:T(8,128)(2,1)}), bf16[64,16,2880]{2,1,0:T(8,128)(2,1)}, u32[]{:S(2)}, u32[]{:S(2)}) %all-to-all-start) | async-done | bytes 5898272 | tf_op jit(solution)/shard_map/all_to_all | solution.py:117
  330.7 13.5 %fusion.61 = f32[1024,1440]{0,1:T(8,128)S(1)} fusion(bf16[1024,2880]{1,0:T(8,128)(2,1)} %bitcast.22, bf16[1,2880,1440]{1,2,0:T(8,128)(2,1)} %param.20), kind=kOutput, calls=%fused_computation.89 | convolution fusion | flops 8493465600 | bytes 20090880 | tf_op jit(solution)/shard_map/dot_general | solution.py:122
  344.3 10.0 %fusion.19 = f32[1024,2880]{0,1:T(8,128)} fusion(f32[1024,1440]{0,1:T(8,128)S(1)} %fusion.61, bf16[1,720,2880]{2,1,0:T(8,128)(2,1)} %param.21), kind=kOutput, calls=%fused_computation.27 | convolution fusion | flops 4252631040 | bytes 21841920 | tf_op jit(solution)/shard_map/dot_general | solution.py:126
  354.3 15.1 %fusion.72 = f32[1024,1440]{0,1:T(8,128)} fusion(bf16[1024,2880]{1,0:T(8,128)(2,1)} %bitcast.22, bf16[2880,1440]{0,1:T(8,128)(2,1)} %collective-permute-done), kind=kOutput, calls=%fused_computation.100 | convolution fusion | flops 8493465600 | bytes 20090880 | tf_op jit(solution)/shard_map/dot_general | solution.py:122
  369.4 14.8 %add_convert_fusion = bf16[1024,2880]{0,1:T(8,128)(2,1)} fusion(f32[1024,2880]{0,1:T(8,128)} %fusion.19, bf16[720,2880]{1,0:T(8,128)(2,1)} %collective-permute-done.1, f32[1024,1440]{0,1:T(8,128)} %fusion.72), kind=kOutput, calls=%fused_computation.4 | convolution fusion | flops 4258529280 | bytes 27740160 | tf_op jit(solution)/shard_map/dot_general | solution.py:126
  384.2 8.5 %copy.39 = bf16[1024,2880]{1,0:T(8,128)(2,1)} copy(bf16[1024,2880]{0,1:T(8,128)(2,1)} %add_convert_fusion) | data formatting | bytes 11796480 | tf_op jit(solution)/shard_map/convert_element_type | solution.py:128
  392.7 6.7 %all-to-all-start.1 = ((bf16[64,16,2880]{2,1,0:T(8,128)(2,1)}), bf16[64,16,2880]{2,1,0:T(8,128)(2,1)}, u32[]{:S(2)}, u32[]{:S(2)}) async-start(bf16[64,16,2880]{2,1,0:T(8,128)(2,1)} %bitcast.94), calls=%async_computation.1 | async-start | bytes 12058624 | tf_op jit(solution)/shard_map/all_to_all | solution.py:129
  399.4 91.4 %all-to-all-done.1 = bf16[64,16,2880]{2,1,0:T(8,128)(2,1)} async-done(((bf16[64,16,2880]{2,1,0:T(8,128)(2,1)}), bf16[64,16,2880]{2,1,0:T(8,128)(2,1)}, u32[]{:S(2)}, u32[]{:S(2)}) %all-to-all-start.1) | async-done | bytes 5898272 | tf_op jit(solution)/shard_map/all_to_all | solution.py:129
  490.8 5.2 %convolution_bitcast_fusion = f32[128,2880]{0,1:T(8,128)S(1)} fusion(bf16[64,16,2880]{2,1,0:T(8,128)(2,1)} %all-to-all-done.1, f32[64,128]{1,0:T(8,128)S(1)} %bitcast.98, s32[64,128]{1,0:T(8,128)S(1)} %convolution_convert_fusion.1, pred[64,128]{1,0:T(8,128)(4,1)S(1)} %bitcast.101), kind=kOutput, calls=%fused_computation.11 | convolution fusion | flops 755892224 | bytes 7446528 | tf_op jit(solution)/shard_map/st,sd->td/dot_general | solution.py:134
  496.0 5.9 %fusion.10 = bf16[1,128,2880]{1,2,0:T(8,128)(2,1)} fusion(f32[128,2880]{0,1:T(8,128)S(1)} %get-tuple-element.8, f32[128,2880]{0,1:T(8,128)S(1)} %convolution_bitcast_fusion, bf16[64,16,2880]{2,1,0:T(8,128)(2,1)} %all-to-all-done.1, f32[64,128]{1,0:T(8,128)S(1)} %bitcast.99, s32[64,128]{1,0:T(8,128)S(1)} %convolution_convert_fusion.1, ...), kind=kOutput, calls=%fused_computation.16 | convolution fusion | flops 756473856 | bytes 9658368 | tf_op jit(solution)/shard_map/st,sd->td/dot_general | solution.py:132
  (27 shorter events, 2.1 us)
Async XLA Ops:
  6.5 51.5 %all-gather.3.cloned.1.call-start = ((), (), s32[]{:S(2)}) async-start(), calls=%async_computation.2 | async-start | bytes 1179648 | tf_op jit(solution)/shard_map/all_gather | solution.py:34
  8.1 206.2 %all-gather.5.cloned.1.call-start = ((), (), s32[]{:S(2)}) async-start(), calls=%async_computation.3 | async-start | bytes 13271040 | tf_op jit(solution)/shard_map/all_gather | solution.py:82
  69.1 145.3 %copy-start.3 = (bf16[1,128,2880]{1,2,0:T(8,128)(2,1)S(1)}, bf16[1,128,2880]{1,2,0:T(8,128)(2,1)}, u32[]{:S(2)}) copy-start(bf16[1,128,2880]{1,2,0:T(8,128)(2,1)} %param.14) | copy-start | bytes 2211844
  214.3 6.2 %copy-start = (f32[2880]{0:T(1024)S(1)}, f32[2880]{0:T(1024)}, u32[]{:S(2)}) copy-start(f32[2880]{0:T(1024)} %param.16) | copy-start | bytes 34564
  233.1 97.6 %all-to-all-start = ((bf16[64,16,2880]{2,1,0:T(8,128)(2,1)}), bf16[64,16,2880]{2,1,0:T(8,128)(2,1)}, u32[]{:S(2)}, u32[]{:S(2)}) async-start(bf16[64,16,2880]{2,1,0:T(8,128)(2,1)} %bitcast.93), calls=%async_computation | async-start | bytes 12058624 | tf_op jit(solution)/shard_map/all_to_all | solution.py:117
  241.2 113.1 %collective-permute-start = (bf16[2880,1440]{0,1:T(8,128)(2,1)}, bf16[2880,1440]{0,1:T(8,128)(2,1)}, u32[]{:S(2)}, u32[]{:S(2)}) collective-permute-start(bf16[2880,1440]{0,1:T(8,128)(2,1)} %bitcast.108), channel_id=1, source_target_pairs={{0,1},{1,0},{2,3},{3,2},{4,5},{5,4},{6,7},{7,6},{8,9},{9,8},{10,11... | collective-permute-start | bytes 24883208 | tf_op jit(solution)/shard_map/ppermute | solution.py:77
  241.3 128.1 %collective-permute-start.1 = (bf16[720,2880]{1,0:T(8,128)(2,1)}, bf16[720,2880]{1,0:T(8,128)(2,1)}, u32[]{:S(2)}, u32[]{:S(2)}) collective-permute-start(bf16[720,2880]{1,0:T(8,128)(2,1)} %bitcast.109), channel_id=1, source_target_pairs={{0,1},{1,0},{2,3},{3,2},{4,5},{5,4},{6,7},{7,6},{8,9},{9,8},{10,11... | collective-permute-start | bytes 12441608 | tf_op jit(solution)/shard_map/ppermute | solution.py:78
  392.7 6.7 %copy-start.1 = (s32[1,128,4]{1,2,0:T(4,128)S(1)}, s32[1,128,4]{1,2,0:T(4,128)}, u32[]{:S(2)}) copy-start(s32[1,128,4]{1,2,0:T(4,128)} %param.18) | copy-start | bytes 6148
  392.7 6.7 %copy-start.2 = (f32[1,128,4]{1,2,0:T(4,128)S(1)}, f32[1,128,4]{1,2,0:T(4,128)}, u32[]{:S(2)}) copy-start(f32[1,128,4]{1,2,0:T(4,128)} %param.19) | copy-start | bytes 6148
  392.7 98.1 %all-to-all-start.1 = ((bf16[64,16,2880]{2,1,0:T(8,128)(2,1)}), bf16[64,16,2880]{2,1,0:T(8,128)(2,1)}, u32[]{:S(2)}, u32[]{:S(2)}) async-start(bf16[64,16,2880]{2,1,0:T(8,128)(2,1)} %bitcast.94), calls=%async_computation.1 | async-start | bytes 12058624 | tf_op jit(solution)/shard_map/all_to_all | solution.py:129
Sparse Core Ops, SparseCore 0:
  9.7 48.3 all-gather.2
  60.2 154.0 all-gather.4
where the time goes:
time: 510 us; the launch traced here: 509 us
  waiting for transfers between devices  366 us (72%)
  matrix products  90.2 us (18%)
  local copies, waits for them, and re-layouts  19.9 us (4%)
  starting transfers between devices  15.5 us (3%)
  between operations  13.6 us (3%)
    all_gather x1, waiting for transfers between devices, local(): lax.all_gather(out_weight, CTX, axis=0, tiled=True)  140 us
    all_to_all x1, waiting for transfers between devices, local(): lax.all_to_all(result.reshape(EXPERTS, CAP, D), CHIPS, split_axis=0, conc...  91.4 us
    all_to_all x1, waiting for transfers between devices, local(): lax.all_to_all(outgoing.reshape(EXPERTS, CAP, D), CHIPS, split_axis=0, co...  88.9 us
    all_gather x1, waiting for transfers between devices, attention(): lax.all_gather(jnp.concatenate([key_rows[0], value_matrix[0]], axis=1), C...  45 us
    dot_general x2, matrix products, half(): gate_up_out = jnp.dot(rows, gate_up, preferred_element_type=jnp.float32)  28.7 us
    dot_general x2, matrix products, half(): return jnp.dot(act, down, preferred_element_type=jnp.float32)  24.8 us
  transfers between devices with their start and end apart: 6, of which 4 were waited for; matrix products, arithmetic and copies ran while one was open for 12% of the time, Pallas kernels for 0%

commit v1 on v0

--- a/solution.py
+++ b/solution.py
@@ -1,3 +1,4 @@
+import functools
 import jax
 import jax.numpy as jnp
 from jax import lax
@@ -14,6 +15,21 @@
 EXP = ("y_lo", "z", "core")
 CHIPS = ("y_hi", "x", "y_lo", "z")
 negative_large = -1e30
+
+
+def manage_loops_now(patch, axis_name):
+    return jnp.concatenate(
+        lax.all_to_all(
+            jnp.stack([patch for _ in range(lax.psum(1, axis_name=axis_name))], axis=0),
+            axis_name,
+            0,
+            0,
+        ),
+        0,
+    )
+
+
+streams_view = functools.partial(manage_loops_now, axis_name=CTX)
 
 
 def attention(queries, key_rows, value_matrix, block_order):
@@ -77,11 +93,7 @@
     gate_up_oth = lax.ppermute(gate_up_own, "core", swap)
     down_oth = lax.ppermute(down_own, "core", swap)
     attended = attention(queries, key_rows, value_matrix, block_order)
-    projected = jnp.dot(
-        attended,
-        lax.all_gather(out_weight, CTX, axis=0, tiled=True),
-        preferred_element_type=jnp.float32,
-    )
+    projected = jnp.dot(attended, streams_view(out_weight), preferred_element_type=jnp.float32)
     residual = (hidden[0].astype(jnp.float32) + projected).astype(jnp.bfloat16)
     res_float = residual.astype(jnp.float32)
     moe_in = (

time: 510 us -> 529 us (1.037)
  waiting for transfers between devices: 366 us -> 337 us
  starting transfers between devices: 15.5 us -> 43.9 us
  local copies, waits for them, and re-layouts: 19.9 us -> 41.6 us
    all_gather x1 -> x0, waiting for transfers between devices: 140 us -> none  [local(): lax.all_gather(out_weight, CTX, axis=0, tiled=True)]
    all_gather x1, waiting for transfers between devices: 45 us -> 158 us  [attention(): lax.all_gather(jnp.concatenate([key_rows[0], value_matrix[0]], axis=1), C...]
    all_to_all x1, starting transfers between devices: 8.18 us -> 29 us  [local(): lax.all_to_all(outgoing.reshape(EXPERTS, CAP, D), CHIPS, split_axis=0, co...]
    all_to_all x0 -> x1, local copies, waits for them, and re-layouts: none -> 16.2 us  [manage_loops_now(): lax.all_to_all(jnp.stack([patch for _ in range(lax.psum(1, axis_name=axis...]
    all_to_all x0 -> x1, starting transfers between devices: none -> 7.6 us  [manage_loops_now(): lax.all_to_all(jnp.stack([patch for _ in range(lax.psum(1, axis_name=axis...]
    another operation x0 -> x1, local copies, waits for them, and re-layouts: none -> 6.55 us  [manage_loops_now(): jnp.stack([patch for _ in range(lax.psum(1, axis_name=axis_name))], axis=0)]
  transfers between devices with their start and end apart: 6 -> 6, of which waited for: 4 -> 4; matrix products, arithmetic and copies ran while one was open for 12% -> 11% of each run, Pallas kernels for 0% -> 0%
where the time goes in v1:
time: 529 us; the launch traced here: 528 us
  waiting for transfers between devices  337 us (64%)
  matrix products  90.4 us (17%)
  starting transfers between devices  43.9 us (8%)
  local copies, waits for them, and re-layouts  41.6 us (8%)
  between operations  13.6 us (3%)
    all_gather x1, waiting for transfers between devices, attention(): lax.all_gather(jnp.concatenate([key_rows[0], value_matrix[0]], axis=1), C...  158 us
    all_to_all x1, waiting for transfers between devices, local(): lax.all_to_all(result.reshape(EXPERTS, CAP, D), CHIPS, split_axis=0, conc...  88.8 us
    all_to_all x1, waiting for transfers between devices, local(): lax.all_to_all(outgoing.reshape(EXPERTS, CAP, D), CHIPS, split_axis=0, co...  87.7 us
    all_to_all x1, starting transfers between devices, local(): lax.all_to_all(outgoing.reshape(EXPERTS, CAP, D), CHIPS, split_axis=0, co...  29 us
    dot_general x2, matrix products, half(): gate_up_out = jnp.dot(rows, gate_up, preferred_element_type=jnp.float32)  28.7 us
    dot_general x2, matrix products, half(): return jnp.dot(act, down, preferred_element_type=jnp.float32)  24.8 us
    all_to_all x1, local copies, waits for them, and re-layouts, manage_loops_now(): lax.all_to_all(jnp.stack([patch for _ in range(lax.psum(1, axis_name=axis...  16.2 us
  transfers between devices with their start and end apart: 6, of which 4 were waited for; matrix products, arithmetic and copies ran while one was open for 11% of the time, Pallas kernels for 0%

profile of v1, /device:TPU:98, one launch (start us, length us, event | category | flops | bytes accessed | tf_op | source)
XLA Modules:
  0.0 527.6 jit_solution(5914609427373871652)
XLA Ops:
  6.5 6.5 %stack.2 = bf16[8,256,2880]{1,2,0:T(8,128)(2,1)} broadcast(bf16[256,2880]{0,1:T(8,128)(2,1)} %param.15), dimensions={1,2} | broadcast | bytes 13271040 | tf_op jit(solution)/shard_map/stack | solution.py:23
  13.1 7.6 %all-to-all-start = ((bf16[8,256,2880]{1,2,0:T(8,128)(2,1)}), bf16[8,256,2880]{1,2,0:T(8,128)(2,1)}, u32[]{:S(2)}, u32[]{:S(2)}) async-start(bf16[8,256,2880]{1,2,0:T(8,128)(2,1)} %stack.2), calls=%async_computation | async-start | bytes 23592960 | tf_op jit(solution)/shard_map/all_to_all | solution.py:22
  20.7 0.7 pad_maximum_fusion
  22.7 158.2 %all-gather.2.cloned.1.call-done = bf16[1024,512]{1,0:T(8,128)(2,1)} async-done(((bf16[128,512]{1,0:T(8,128)(2,1)}), bf16[1024,512]{1,0:T(8,128)(2,1)}) %all-gather.2.cloned.1.call-update) | async-done | bytes 1048592 | tf_op jit(solution)/shard_map/all_gather | solution.py:50
  180.8 1.5 copy.45
  182.3 9.6 %fusion.71 = (f32[4,8,128]{2,1,0:T(8,128)S(1)}, bf16[4,8,128,1024]{2,3,1,0:T(8,128)(2,1)}) fusion(pred[128,1024]{0,1:T(8,128)(4,1)S(1)} %broadcast_compare_fusion, bf16[128,4,8,64]{0,3,2,1:T(8,128)(2,1)S(1)} %bitcast.100, bf16[1024,2,4,64]{0,3,2,1:T(8,128)(2,1)S(1)} %bitcast.97), kind=kOutput, calls=%fused_computation.99 | convolution fusion | flops 562037760 | bytes 9715712 | tf_op jit(solution)/shard_map/sub | solution.py:63
  192.0 4.9 fusion.32
  196.9 2.0 all-to-all-done
  198.9 16.2 %copy.48 = bf16[8,256,2880]{2,1,0:T(8,128)(2,1)} copy(bf16[8,256,2880]{1,2,0:T(8,128)(2,1)} %all-to-all-done) | data formatting | bytes 23592960 | tf_op jit(solution)/shard_map/all_to_all | solution.py:22
  215.2 7.1 %multiply_reduce_fusion = (f32[128]{0:T(128)S(1)}, f32[128,2880]{0,1:T(8,128)S(1)}) fusion(bf16[128,2048]{0,1:T(8,128)(2,1)S(1)} %bitcast.99, bf16[2048,2880]{1,0:T(8,128)(2,1)} %bitcast.94, bf16[1,128,2880]{1,2,0:T(8,128)(2,1)S(1)} %copy-done), kind=kOutput, calls=%fused_computation.33 | convolution fusion | flops 1512161152 | bytes 14533120 | tf_op jit(solution)/shard_map/dot_general | solution.py:96
  222.3 4.0 convolution_convert_fusion
  226.3 8.5 %copy.49 = bf16[1024,2880]{1,0:T(8,128)(2,1)} copy(bf16[1024,2880]{0,1:T(8,128)(2,1)} %convolution_convert_fusion) | data formatting | bytes 11796480 | tf_op jit(solution)/shard_map/convert_element_type | solution.py:128
  234.8 29.0 %all-to-all-start.1 = ((bf16[64,16,2880]{2,1,0:T(8,128)(2,1)}), bf16[64,16,2880]{2,1,0:T(8,128)(2,1)}, u32[]{:S(2)}, u32[]{:S(2)}) async-start(bf16[64,16,2880]{2,1,0:T(8,128)(2,1)} %bitcast.95), calls=%async_computation.1 | async-start | bytes 12058624 | tf_op jit(solution)/shard_map/all_to_all | solution.py:129
  263.9 0.5 collective-permute-start.1
  264.4 87.7 %all-to-all-done.1 = bf16[64,16,2880]{2,1,0:T(8,128)(2,1)} async-done(((bf16[64,16,2880]{2,1,0:T(8,128)(2,1)}), bf16[64,16,2880]{2,1,0:T(8,128)(2,1)}, u32[]{:S(2)}, u32[]{:S(2)}) %all-to-all-start.1) | async-done | bytes 5898272 | tf_op jit(solution)/shard_map/all_to_all | solution.py:129
  352.1 13.5 %fusion.61 = f32[1024,1440]{0,1:T(8,128)S(1)} fusion(bf16[1024,2880]{1,0:T(8,128)(2,1)} %bitcast.23, bf16[1,2880,1440]{1,2,0:T(8,128)(2,1)} %param.20), kind=kOutput, calls=%fused_computation.89 | convolution fusion | flops 8493465600 | bytes 20090880 | tf_op jit(solution)/shard_map/dot_general | solution.py:134
  365.7 10.0 %fusion.19 = f32[1024,2880]{0,1:T(8,128)} fusion(f32[1024,1440]{0,1:T(8,128)S(1)} %fusion.61, bf16[1,720,2880]{2,1,0:T(8,128)(2,1)} %param.21), kind=kOutput, calls=%fused_computation.27 | convolution fusion | flops 4252631040 | bytes 21841920 | tf_op jit(solution)/shard_map/dot_general | solution.py:138
  375.7 15.1 %fusion.72 = f32[1024,1440]{0,1:T(8,128)} fusion(bf16[1024,2880]{1,0:T(8,128)(2,1)} %bitcast.23, bf16[2880,1440]{0,1:T(8,128)(2,1)} %collective-permute-done), kind=kOutput, calls=%fused_computation.100 | convolution fusion | flops 8493465600 | bytes 20090880 | tf_op jit(solution)/shard_map/dot_general | solution.py:134
  390.8 14.8 %add_convert_fusion = bf16[1024,2880]{0,1:T(8,128)(2,1)} fusion(f32[1024,2880]{0,1:T(8,128)} %fusion.19, bf16[720,2880]{1,0:T(8,128)(2,1)} %collective-permute-done.1, f32[1024,1440]{0,1:T(8,128)} %fusion.72), kind=kOutput, calls=%fused_computation.4 | convolution fusion | flops 4258529280 | bytes 27740160 | tf_op jit(solution)/shard_map/dot_general | solution.py:138
  405.6 8.5 %copy.50 = bf16[1024,2880]{1,0:T(8,128)(2,1)} copy(bf16[1024,2880]{0,1:T(8,128)(2,1)} %add_convert_fusion) | data formatting | bytes 11796480 | tf_op jit(solution)/shard_map/convert_element_type | solution.py:140
  414.1 6.7 %all-to-all-start.2 = ((bf16[64,16,2880]{2,1,0:T(8,128)(2,1)}), bf16[64,16,2880]{2,1,0:T(8,128)(2,1)}, u32[]{:S(2)}, u32[]{:S(2)}) async-start(bf16[64,16,2880]{2,1,0:T(8,128)(2,1)} %bitcast.96), calls=%async_computation.2 | async-start | bytes 12058624 | tf_op jit(solution)/shard_map/all_to_all | solution.py:141
  420.8 88.8 %all-to-all-done.2 = bf16[64,16,2880]{2,1,0:T(8,128)(2,1)} async-done(((bf16[64,16,2880]{2,1,0:T(8,128)(2,1)}), bf16[64,16,2880]{2,1,0:T(8,128)(2,1)}, u32[]{:S(2)}, u32[]{:S(2)}) %all-to-all-start.2) | async-done | bytes 5898272 | tf_op jit(solution)/shard_map/all_to_all | solution.py:141
  509.6 5.2 convolution_bitcast_fusion
  514.8 5.9 %fusion.12 = bf16[1,128,2880]{1,2,0:T(8,128)(2,1)} fusion(f32[128,2880]{0,1:T(8,128)S(1)} %get-tuple-element.8, f32[128,2880]{0,1:T(8,128)S(1)} %convolution_bitcast_fusion, bf16[64,16,2880]{2,1,0:T(8,128)(2,1)} %all-to-all-done.2, f32[64,128]{1,0:T(8,128)S(1)} %bitcast.102, s32[64,128]{1,0:T(8,128)S(1)} %convolution_convert_fusion.1, ...), kind=kOutput, calls=%fused_computation.19 | convolution fusion | flops 756473856 | bytes 9658368 | tf_op jit(solution)/shard_map/st,sd->td/dot_general | solution.py:144
  (36 shorter events, 1.3 us)
Async XLA Ops:
  13.1 7.6 %copy-start.2 = (bf16[1,128,256]{2,1,0:T(8,128)(2,1)S(1)}, bf16[1,128,256]{2,1,0:T(8,128)(2,1)}, u32[]{:S(2)}) copy-start(bf16[1,128,256]{2,1,0:T(8,128)(2,1)} %param.13) | copy-start | bytes 196612
  13.1 7.6 %copy-start.3 = (bf16[1,128,256]{2,1,0:T(8,128)(2,1)S(1)}, bf16[1,128,256]{2,1,0:T(8,128)(2,1)}, u32[]{:S(2)}) copy-start(bf16[1,128,256]{2,1,0:T(8,128)(2,1)} %param.12) | copy-start | bytes 196612
  13.1 8.4 %copy-start.1 = (bf16[1,128,2048]{2,1,0:T(8,128)(2,1)S(1)}, bf16[1,128,2048]{2,1,0:T(8,128)(2,1)}, u32[]{:S(2)}) copy-start(bf16[1,128,2048]{2,1,0:T(8,128)(2,1)} %param.11) | copy-start | bytes 1572868
  13.1 8.7 %copy-start.5 = (s32[1,128,4]{1,2,0:T(4,128)S(1)}, s32[1,128,4]{1,2,0:T(4,128)}, u32[]{:S(2)}) copy-start(s32[1,128,4]{1,2,0:T(4,128)} %param.18) | copy-start | bytes 6148
  13.1 9.1 %copy-start.7 = (s32[16]{0:T(128)S(1)}, s32[16]{0:T(128)}, u32[]{:S(2)}) copy-start(s32[16]{0:T(128)} %param.17) | copy-start | bytes 196
  13.1 185.8 %all-to-all-start = ((bf16[8,256,2880]{1,2,0:T(8,128)(2,1)}), bf16[8,256,2880]{1,2,0:T(8,128)(2,1)}, u32[]{:S(2)}, u32[]{:S(2)}) async-start(bf16[8,256,2880]{1,2,0:T(8,128)(2,1)} %stack.2), calls=%async_computation | async-start | bytes 23592960 | tf_op jit(solution)/shard_map/all_to_all | solution.py:22
  20.7 160.1 %all-gather.2.cloned.1.call-start = ((), (), s32[]{:S(2)}) async-start(), calls=%async_computation.3 | async-start | bytes 1179648 | tf_op jit(solution)/shard_map/all_gather | solution.py:50
  196.9 18.2 %copy-start = (bf16[1,128,2880]{1,2,0:T(8,128)(2,1)S(1)}, bf16[1,128,2880]{1,2,0:T(8,128)(2,1)}, u32[]{:S(2)}) copy-start(bf16[1,128,2880]{1,2,0:T(8,128)(2,1)} %param.14) | copy-start | bytes 2211844
  215.2 7.1 %copy-start.4 = (f32[2880]{0:T(1024)S(1)}, f32[2880]{0:T(1024)}, u32[]{:S(2)}) copy-start(f32[2880]{0:T(1024)} %param.16) | copy-start | bytes 34564
  234.8 117.3 %all-to-all-start.1 = ((bf16[64,16,2880]{2,1,0:T(8,128)(2,1)}), bf16[64,16,2880]{2,1,0:T(8,128)(2,1)}, u32[]{:S(2)}, u32[]{:S(2)}) async-start(bf16[64,16,2880]{2,1,0:T(8,128)(2,1)} %bitcast.95), calls=%async_computation.1 | async-start | bytes 12058624 | tf_op jit(solution)/shard_map/all_to_all | solution.py:129
  263.8 111.8 %collective-permute-start = (bf16[2880,1440]{0,1:T(8,128)(2,1)}, bf16[2880,1440]{0,1:T(8,128)(2,1)}, u32[]{:S(2)}, u32[]{:S(2)}) collective-permute-start(bf16[2880,1440]{0,1:T(8,128)(2,1)} %bitcast.111), channel_id=1, source_target_pairs={{0,1},{1,0},{2,3},{3,2},{4,5},{5,4},{6,7},{7,6},{8,9},{9,8},{10,11... | collective-permute-start | bytes 24883208 | tf_op jit(solution)/shard_map/ppermute | solution.py:93
  263.9 126.9 %collective-permute-start.1 = (bf16[720,2880]{1,0:T(8,128)(2,1)}, bf16[720,2880]{1,0:T(8,128)(2,1)}, u32[]{:S(2)}, u32[]{:S(2)}) collective-permute-start(bf16[720,2880]{1,0:T(8,128)(2,1)} %bitcast.112), channel_id=1, source_target_pairs={{0,1},{1,0},{2,3},{3,2},{4,5},{5,4},{6,7},{7,6},{8,9},{9,8},{10,11... | collective-permute-start | bytes 12441608 | tf_op jit(solution)/shard_map/ppermute | solution.py:94
  414.1 6.7 %copy-start.6 = (f32[1,128,4]{1,2,0:T(4,128)S(1)}, f32[1,128,4]{1,2,0:T(4,128)}, u32[]{:S(2)}) copy-start(f32[1,128,4]{1,2,0:T(4,128)} %param.19) | copy-start | bytes 6148
  414.1 95.5 %all-to-all-start.2 = ((bf16[64,16,2880]{2,1,0:T(8,128)(2,1)}), bf16[64,16,2880]{2,1,0:T(8,128)(2,1)}, u32[]{:S(2)}, u32[]{:S(2)}) async-start(bf16[64,16,2880]{2,1,0:T(8,128)(2,1)} %bitcast.96), calls=%async_computation.2 | async-start | bytes 12058624 | tf_op jit(solution)/shard_map/all_to_all | solution.py:141
Sparse Core Ops, SparseCore 0:
  23.9 156.9 all-gather.1
